TPU v7x, 512 devices: a whole 4x8x8 slice. The times are simulated.
512 devices in a mesh: dp: 2 (over core), seq: 64 (over y, z), tensor: 4 (over x).
Axes of the slice: x: 4, y: 8, z: 8, core: 2. Of those that a mesh axis runs over, the one named last changes fastest.
Arguments:
- query: bfloat16 [2, 16384, 2048], P('dp', 'seq', 'tensor'), may hold values from -1.75 to 1.75
- key_rows: bfloat16 [2, 16384, 2048], P('dp', 'seq', 'tensor'), may hold values from -1.75 to 1.75
- value: bfloat16 [2, 16384, 2048], P('dp', 'seq', 'tensor'), may hold values from -40 to 40
- gain: float32 [2048], P('tensor'), may hold values from 0.25 to 1.75
- grad_out: bfloat16 [2, 16384, 2048], P('dp', 'seq', 'tensor'), may hold values from -16 to 16
- start_offset: int32 [2, 256], P('dp', 'seq'), may hold values from 0 to 64, as said below
Outputs:
- attn_out: bfloat16 [2, 16384, 2048], P('dp', 'seq', 'tensor')
- grad_query: bfloat16 [2, 16384, 2048], P('dp', 'seq', 'tensor')
- grad_key: bfloat16 [2, 16384, 2048], P('dp', 'seq', 'tensor')
- grad_value: bfloat16 [2, 16384, 2048], P('dp', 'seq', 'tensor')
- grad_gain: float32 [2048], P('tensor')
Inputs may be any that keep to these rules, and one draw needn't show every extreme that they name: `start_offset`: the position within its block of 64 positions at which a document starts; 64 when none starts in the block; every sequence begins a document at its first position.
All inputs are finite; a program needn't handle non-finite values.
Results may differ from a plain program's by a relative error of at most 0.0058.
Values sent between devices are 32-bit elements; how exact they have to be, the bound alone decides.
No kernel may reach another device: no remote copies, remote signals or barrier semaphores. Data moves between devices by JAX's collectives and lax.ppermute only.
A program may use at most 64 MiB of HBM per device.

v0:
```python
import jax
import jax.numpy as jnp
from jax import lax
from jax.sharding import PartitionSpec as P

DH = 128
BLK = 64
CH = 2048
eps_value = 1e-05


def carried_in(part, axis, combine, identity, reverse):
    count = lax.axis_size(axis)
    place = lax.axis_index(axis)
    ahead = count - 1 - place if reverse else place
    gathered = jax.tree.map(lambda a: lax.all_gather(a, axis), part)
    state = jax.tree.map(lambda a, e: jnp.zeros_like(a) + jnp.asarray(e, a.dtype), part, identity)

    def one(turn, state):
        source = count - 1 - turn if reverse else turn
        return combine(
            state, jax.tree.map(lambda a: lax.dynamic_index_in_dim(a, source, 0, False), gathered)
        )

    return lax.fori_loop(0, ahead, one, state)


def segment_rows(offsets, length_dev):
    positions = jnp.arange(length_dev, dtype=jnp.int32)
    block_starts = jnp.arange(offsets.shape[0], dtype=jnp.int32) * BLK + offsets
    present = offsets < BLK
    covered = (block_starts[None, :] <= positions[:, None]) & present[None, :]
    labels = jnp.sum(covered.astype(jnp.int32), axis=1)
    allowed = (labels[:, None] == labels[None, :]) & (positions[None, :] <= positions[:, None])
    starts = jnp.sum(present.astype(jnp.int32))
    return (labels, starts, allowed)


def joined(earlier, later):
    return (
        jnp.where(later[1] > 0, later[0], earlier[0] + later[0]),
        jnp.maximum(earlier[1], later[1]),
    )


def shards(query, key_rows, value, gain, grad_out, start_offset):
    length_dev = query.shape[1]
    width_local = query.shape[2]
    heads_local = width_local // DH
    query_heads = query[0].reshape(length_dev, heads_local, DH)
    key_heads = key_rows[0].reshape(length_dev, heads_local, DH)
    value_heads = value[0].reshape(length_dev, heads_local, DH)
    labels, starts, allowed = segment_rows(start_offset[0], length_dev)
    head_mask = (labels == 0)[:, None, None]
    tail_mask = (labels == starts)[:, None, None]
    reset = (starts > 0).astype(jnp.int32)
    scores = jnp.einsum("thd,shd->hts", query_heads, key_heads, preferred_element_type=jnp.float32)
    weights = jnp.where(allowed[None], scores, 0.0).astype(jnp.bfloat16)
    local_out = jnp.einsum("hts,shd->thd", weights, value_heads, preferred_element_type=jnp.float32)
    tail_keys = jnp.where(tail_mask, key_heads, jnp.zeros_like(key_heads))
    tail_values = jnp.where(tail_mask, value_heads, jnp.zeros_like(value_heads))
    tail_state = jnp.einsum(
        "shi,shj->hij", tail_keys, value_heads, preferred_element_type=jnp.float32
    )
    zero_state = jnp.zeros_like(tail_state)
    incoming = carried_in((tail_state, reset), "seq", joined, (zero_state, jnp.int32(0)), False)[0]
    carried = incoming.astype(jnp.bfloat16)
    head_query = jnp.where(head_mask, query_heads, jnp.zeros_like(query_heads))
    carried_out = jnp.einsum(
        "thi,hij->thj", head_query, carried, preferred_element_type=jnp.float32
    )
    attended = (local_out + carried_out).reshape(length_dev, width_local)
    upstream = grad_out[0].astype(jnp.float32)
    scaled = gain[None, :] * upstream
    square_local = jnp.sum(attended * attended, axis=1)
    square_total = lax.psum(square_local, "tensor")
    inverse = lax.rsqrt(square_total / CH + eps_value)
    normed = attended * inverse[:, None]
    product_total = lax.psum(jnp.sum(scaled * normed, axis=1), "tensor")
    output = (gain[None, :] * normed).astype(jnp.bfloat16)
    grad_pre = (inverse[:, None] * (scaled - normed * (product_total / CH)[:, None])).astype(
        jnp.bfloat16
    )
    gain_local = jnp.sum(upstream * normed, axis=0)
    grad_gain = lax.psum(gain_local, ("dp", "seq"))
    grad_heads = grad_pre.reshape(length_dev, heads_local, DH)
    grad_state = jnp.einsum(
        "thi,thj->hij", head_query, grad_heads, preferred_element_type=jnp.float32
    )
    later = carried_in((grad_state, reset), "seq", joined, (zero_state, jnp.int32(0)), True)[0]
    later_half = later.astype(jnp.bfloat16)
    grad_scores = jnp.einsum(
        "thd,shd->hts", grad_heads, value_heads, preferred_element_type=jnp.float32
    )
    grad_weights = jnp.where(allowed[None], grad_scores, 0.0).astype(jnp.bfloat16)
    head_grad = jnp.where(head_mask, grad_heads, jnp.zeros_like(grad_heads))
    grad_query = jnp.einsum(
        "hts,shd->thd", grad_weights, key_heads, preferred_element_type=jnp.float32
    ) + jnp.einsum("thj,hij->thi", head_grad, carried, preferred_element_type=jnp.float32)
    grad_key = jnp.einsum(
        "hts,thd->shd", grad_weights, query_heads, preferred_element_type=jnp.float32
    ) + jnp.einsum("shj,hij->shi", tail_values, later_half, preferred_element_type=jnp.float32)
    grad_value = jnp.einsum(
        "hts,thd->shd", weights, grad_heads, preferred_element_type=jnp.float32
    ) + jnp.einsum("shi,hij->shj", tail_keys, later_half, preferred_element_type=jnp.float32)
    shape_dev = (1, length_dev, width_local)
    return (
        output.reshape(shape_dev),
        grad_query.reshape(shape_dev).astype(jnp.bfloat16),
        grad_key.reshape(shape_dev).astype(jnp.bfloat16),
        grad_value.reshape(shape_dev).astype(jnp.bfloat16),
        grad_gain,
    )


def solution(mesh):
    return jax.shard_map(
        shards,
        mesh=mesh,
        in_specs=(
            P("dp", "seq", "tensor"),
            P("dp", "seq", "tensor"),
            P("dp", "seq", "tensor"),
            P("tensor"),
            P("dp", "seq", "tensor"),
            P("dp", "seq"),
        ),
        out_specs=(
            P("dp", "seq", "tensor"),
            P("dp", "seq", "tensor"),
            P("dp", "seq", "tensor"),
            P("dp", "seq", "tensor"),
            P("tensor"),
        ),
        check_vma=False,
    )
```

profile of v0, /device:TPU:1, one launch (start us, length us, event | category | flops | bytes accessed | tf_op | source)
XLA Modules:
  0.0 739.9 jit_solution(13396427716960763037)
XLA Ops:
  7.9 1.3 fusion.29
  9.2 1.1 copy.54
  10.3 1.1 copy.57
  13.8 1.1 copy.53
  14.9 1.1 copy.62
  15.9 1.3 dynamic-slice
  18.0 26.8 %all-reduce = s32[64]{0:T(128)S(1)} all-reduce(s32[64]{0:T(128)S(1)} %dynamic-update-slice), channel_id=1, replica_groups=mesh['dp'=2,'seq'=64,'tensor'=4] {'seq'}, use_global_device_ids=true, to_apply=%add | all-reduce | flops 64 | bytes 512
  45.6 112.6 %all-gather.5.cloned.1.call-done = f32[256,128,128]{2,1,0:T(8,128)} async-done(((f32[4,128,128]{2,1,0:T(8,128)}), f32[256,128,128]{2,1,0:T(8,128)}) %all-gather.5.cloned.1.call-update) | async-done | bytes 16777232 | tf_op jit(solution)/shard_map/all_gather | solution.py:16
  158.5 8.4 %psum.21 = f32[256]{0:T(256)S(1)} all-reduce(f32[256]{0:T(256)S(1)} %get-tuple-element.176), channel_id=1, replica_groups=mesh['dp'=2,'seq'=64,'tensor'=4] {'tensor'}, use_global_device_ids=true, to_apply=%region_5.6 | all-reduce | flops 256 | bytes 2048 | tf_op jit(solution)/shard_map/psum | solution.py:76
  167.1 1.2 fusion.10
  168.3 6.0 psum.22
  178.1 405.6 %psum.23 = f32[512]{0:T(512)} all-reduce(f32[512]{0:T(512)S(1)} %get-tuple-element.150), channel_id=1, replica_groups=mesh['dp'=2,'seq'=64,'tensor'=4] {'dp','seq'}, use_global_device_ids=true, to_apply=%region_11.12 | all-reduce | flops 512 | bytes 4096 | tf_op jit(solution)/shard_map/psum | solution.py:85
  585.0 145.9 %while.27 = (s32[]{:T(128)}, f32[4,128,128]{2,1,0:T(8,128)S(1)}, s32[]{:T(128)}, s32[64]{0:T(128)S(1)}, f32[64,4,128,128]{3,2,1,0:T(8,128)}, /*index=5*/s32[]{:T(128)}, s32[]{:T(128)}, s32[]{:T(128)}, s32[]{:T(128)}, s32[1]{0:T(128)}) while((s32[]{:T(128)}, f32[4,128,128]{2,1,0:T(8,128)S(1)}, s32[]{:T(128)}, s32[64]{0:T(128)S(1)}, ...), condition=%wide.region_9.10_spmd, body=%wide.region_8.9_spmd.sunk | while | flops 131079 | bytes 786613 | solution.py:25
  586.3 1.1 add_select_fusion.5
  588.6 1.1 add_select_fusion.5
  590.9 1.1 add_select_fusion.5
  593.2 1.1 add_select_fusion.5
  595.5 1.1 add_select_fusion.5
  597.9 1.1 add_select_fusion.5
  600.2 1.1 add_select_fusion.5
  602.5 1.1 add_select_fusion.5
  604.8 1.1 add_select_fusion.5
  607.1 1.1 add_select_fusion.5
  609.4 1.1 add_select_fusion.5
  611.8 1.1 add_select_fusion.5
  614.1 1.1 add_select_fusion.5
  616.4 1.1 add_select_fusion.5
  618.7 1.1 add_select_fusion.5
  621.0 1.1 add_select_fusion.5
  623.3 1.1 add_select_fusion.5
  625.7 1.1 add_select_fusion.5
  628.0 1.1 add_select_fusion.5
  630.3 1.1 add_select_fusion.5
  632.6 1.1 add_select_fusion.5
  634.9 1.1 add_select_fusion.5
  637.2 1.1 add_select_fusion.5
  639.5 1.1 add_select_fusion.5
  641.9 1.1 add_select_fusion.5
  644.2 1.1 add_select_fusion.5
  646.5 1.1 add_select_fusion.5
  648.8 1.1 add_select_fusion.5
  651.1 1.1 add_select_fusion.5
  653.4 1.1 add_select_fusion.5
  658.1 1.1 add_select_fusion.5
  662.7 1.1 add_select_fusion.5
  667.3 1.1 add_select_fusion.5
  669.7 1.1 add_select_fusion.5
  672.0 1.1 add_select_fusion.5
  674.3 1.1 add_select_fusion.5
  676.6 1.1 add_select_fusion.5
  678.9 1.1 add_select_fusion.5
  683.5 1.1 add_select_fusion.5
  688.2 1.1 add_select_fusion.5
  692.8 1.1 add_select_fusion.5
  697.4 1.1 add_select_fusion.5
  702.1 1.1 add_select_fusion.5
  706.7 1.1 add_select_fusion.5
  711.3 1.1 add_select_fusion.5
  713.7 1.1 add_select_fusion.5
  716.0 1.1 add_select_fusion.5
  718.3 1.1 add_select_fusion.5
  720.6 1.1 add_select_fusion.5
  722.9 1.1 add_select_fusion.5
  727.5 1.1 add_select_fusion.5
  (112 shorter events, 61.4 us)
Async XLA Ops:
  7.2 576.5 %copy-start = (f32[512]{0:T(512)S(1)}, f32[512]{0:T(512)}, u32[]{:S(2)}) copy-start(f32[512]{0:T(512)} %param.13) | copy-start | bytes 6148
  7.2 151.0 %all-gather.5.cloned.1.call-start = ((), (), s32[]{:S(2)}) async-start(), calls=%async_computation | async-start | bytes 17039360 | tf_op jit(solution)/shard_map/all_gather | solution.py:16
  13.1 571.9 %all-gather.7.cloned.1.call-start = ((), (), s32[]{:S(2)}) async-start(), calls=%async_computation.1 | async-start | bytes 17039360 | tf_op jit(solution)/shard_map/all_gather | solution.py:16
Sparse Core Ops, SparseCore 0:
  13.2 144.9 all-gather.4
  176.2 284.0 all-gather.6
where the time goes:
time: 743 us; the launch traced here: 740 us
  blocking collectives  447 us (60%)
  waiting for transfers between devices  113 us (15%)
  other arithmetic  71.9 us (10%)
  local copies, waits for them, and re-layouts  46.4 us (6%)
  loops' own time  42.6 us (6%)
  between operations  14.9 us (2%)
    psum x1, blocking collectives, shards(): grad_gain = lax.psum(gain_local, ('dp', 'seq'))  406 us
    all_gather x2, waiting for transfers between devices, carried_in(): gathered = jax.tree.map(lambda a: lax.all_gather(a, axis), part)  113 us
    select_n x63, other arithmetic, joined(): jnp.where(later[1] > 0, later[0], earlier[0] + later[0])  66.2 us
    another operation x2, loops' own time, carried_in(): return lax.fori_loop(0, ahead, one, state)  42.6 us
    dynamic_slice x63, local copies, waits for them, and re-layouts, one(): lax.dynamic_index_in_dim(a, source, 0, False)  37.1 us
    unnamed x1, blocking collectives  26.8 us
  transfers between devices with their start and end apart: 2, of which 1 were waited for; matrix products, arithmetic and copies ran while one was open for 1% of the time, Pallas kernels for 0%

commit v1 on v0

--- a/solution.py
+++ b/solution.py
@@ -7,6 +7,12 @@
 BLK = 64
 CH = 2048
 eps_value = 1e-05
+
+
+def indices_state(panel):
+    for to_i in ("seq", "dp"):
+        panel = jax.lax.psum(panel, to_i)
+    return panel
 
 
 def carried_in(part, axis, combine, identity, reverse):
@@ -82,7 +88,7 @@
         jnp.bfloat16
     )
     gain_local = jnp.sum(upstream * normed, axis=0)
-    grad_gain = lax.psum(gain_local, ("dp", "seq"))
+    grad_gain = indices_state(gain_local)
     grad_heads = grad_pre.reshape(length_dev, heads_local, DH)
     grad_state = jnp.einsum(
         "thi,thj->hij", head_query, grad_heads, preferred_element_type=jnp.float32

time: 743 us -> 636 us (0.86)
  blocking collectives: 447 us -> 340 us
    psum x1 -> x2, blocking collectives: 406 us -> 299 us  [indices_state(): panel = jax.lax.psum(panel, to_i)]
where the time goes in v1:
time: 636 us; the launch traced here: 633 us
  blocking collectives  340 us (53%)
  waiting for transfers between devices  113 us (18%)
  other arithmetic  71.9 us (11%)
  local copies, waits for them, and re-layouts  46.4 us (7%)
  loops' own time  42.6 us (7%)
  between operations  14.9 us (2%)
    psum x2, blocking collectives, indices_state(): panel = jax.lax.psum(panel, to_i)  299 us
    all_gather x2, waiting for transfers between devices, carried_in(): gathered = jax.tree.map(lambda a: lax.all_gather(a, axis), part)  113 us
    select_n x63, other arithmetic, joined(): jnp.where(later[1] > 0, later[0], earlier[0] + later[0])  66.2 us
    another operation x2, loops' own time, carried_in(): return lax.fori_loop(0, ahead, one, state)  42.6 us
    dynamic_slice x63, local copies, waits for them, and re-layouts, one(): lax.dynamic_index_in_dim(a, source, 0, False)  37.1 us
    unnamed x1, blocking collectives  26.8 us
  transfers between devices with their start and end apart: 2, of which 1 were waited for; matrix products, arithmetic and copies ran while one was open for 1% of the time, Pallas kernels for 0%

profile of v1, /device:TPU:1, one launch (start us, length us, event | category | flops | bytes accessed | tf_op | source)
XLA Modules:
  0.0 633.0 jit_solution(306783847588512424)
XLA Ops:
  7.9 1.3 fusion.29
  9.2 1.1 copy.54
  10.3 1.1 copy.57
  13.8 1.1 copy.53
  14.9 1.1 copy.62
  15.9 1.3 dynamic-slice
  18.0 26.8 %all-reduce = s32[64]{0:T(128)S(1)} all-reduce(s32[64]{0:T(128)S(1)} %dynamic-update-slice), channel_id=1, replica_groups=mesh['dp'=2,'seq'=64,'tensor'=4] {'seq'}, use_global_device_ids=true, to_apply=%add | all-reduce | flops 64 | bytes 512
  45.6 112.6 %all-gather.5.cloned.1.call-done = f32[256,128,128]{2,1,0:T(8,128)} async-done(((f32[4,128,128]{2,1,0:T(8,128)}), f32[256,128,128]{2,1,0:T(8,128)}) %all-gather.5.cloned.1.call-update) | async-done | bytes 16777232 | tf_op jit(solution)/shard_map/all_gather | solution.py:22
  158.5 8.4 %psum.28 = f32[256]{0:T(256)S(1)} all-reduce(f32[256]{0:T(256)S(1)} %get-tuple-element.176), channel_id=1, replica_groups=mesh['dp'=2,'seq'=64,'tensor'=4] {'tensor'}, use_global_device_ids=true, to_apply=%region_5.6 | all-reduce | flops 256 | bytes 2048 | tf_op jit(solution)/shard_map/psum | solution.py:82
  167.1 1.2 fusion.10
  168.3 6.0 psum.29
  178.1 263.6 %psum.30 = f32[512]{0:T(512)S(1)} all-reduce(f32[512]{0:T(512)S(1)} %get-tuple-element.150), channel_id=1, replica_groups=mesh['dp'=2,'seq'=64,'tensor'=4] {'seq'}, use_global_device_ids=true, to_apply=%region_11.12 | all-reduce | flops 512 | bytes 4096 | tf_op jit(solution)/shard_map/psum | solution.py:14
  441.6 35.1 %psum.31 = f32[512]{0:T(512)} all-reduce(f32[512]{0:T(512)S(1)} %psum.30), channel_id=1, replica_groups=mesh['dp'=2,'seq'=64,'tensor'=4] {'dp'}, use_global_device_ids=true, to_apply=%region_12.13 | all-reduce | flops 512 | bytes 4096 | tf_op jit(solution)/shard_map/psum | solution.py:14
  478.0 145.9 %while.27 = (s32[]{:T(128)}, f32[4,128,128]{2,1,0:T(8,128)S(1)}, s32[]{:T(128)}, s32[64]{0:T(128)S(1)}, f32[64,4,128,128]{3,2,1,0:T(8,128)}, /*index=5*/s32[]{:T(128)}, s32[]{:T(128)}, s32[]{:T(128)}, s32[]{:T(128)}, s32[1]{0:T(128)}) while((s32[]{:T(128)}, f32[4,128,128]{2,1,0:T(8,128)S(1)}, s32[]{:T(128)}, s32[64]{0:T(128)S(1)}, ...), condition=%wide.region_9.10_spmd, body=%wide.region_8.9_spmd.sunk | while | flops 131079 | bytes 786613 | solution.py:31
  479.3 1.1 add_select_fusion.5
  481.6 1.1 add_select_fusion.5
  483.9 1.1 add_select_fusion.5
  486.3 1.1 add_select_fusion.5
  488.6 1.1 add_select_fusion.5
  490.9 1.1 add_select_fusion.5
  493.2 1.1 add_select_fusion.5
  495.5 1.1 add_select_fusion.5
  497.8 1.1 add_select_fusion.5
  500.2 1.1 add_select_fusion.5
  502.5 1.1 add_select_fusion.5
  504.8 1.1 add_select_fusion.5
  507.1 1.1 add_select_fusion.5
  509.4 1.1 add_select_fusion.5
  511.7 1.1 add_select_fusion.5
  514.1 1.1 add_select_fusion.5
  516.4 1.1 add_select_fusion.5
  518.7 1.1 add_select_fusion.5
  521.0 1.1 add_select_fusion.5
  523.3 1.1 add_select_fusion.5
  525.6 1.1 add_select_fusion.5
  527.9 1.1 add_select_fusion.5
  530.3 1.1 add_select_fusion.5
  532.6 1.1 add_select_fusion.5
  534.9 1.1 add_select_fusion.5
  537.2 1.1 add_select_fusion.5
  539.5 1.1 add_select_fusion.5
  541.8 1.1 add_select_fusion.5
  544.2 1.1 add_select_fusion.5
  546.5 1.1 add_select_fusion.5
  548.8 1.1 add_select_fusion.5
  551.1 1.1 add_select_fusion.5
  555.7 1.1 add_select_fusion.5
  560.4 1.1 add_select_fusion.5
  565.0 1.1 add_select_fusion.5
  569.6 1.1 add_select_fusion.5
  574.3 1.1 add_select_fusion.5
  578.9 1.1 add_select_fusion.5
  583.5 1.1 add_select_fusion.5
  585.8 1.1 add_select_fusion.5
  588.2 1.1 add_select_fusion.5
  590.5 1.1 add_select_fusion.5
  592.8 1.1 add_select_fusion.5
  595.1 1.1 add_select_fusion.5
  599.7 1.1 add_select_fusion.5
  604.4 1.1 add_select_fusion.5
  609.0 1.1 add_select_fusion.5
  613.6 1.1 add_select_fusion.5
  618.3 1.1 add_select_fusion.5
  622.9 1.1 add_select_fusion.5
  (113 shorter events, 62.4 us)
Async XLA Ops:
  7.2 469.5 %copy-start = (f32[512]{0:T(512)S(1)}, f32[512]{0:T(512)}, u32[]{:S(2)}) copy-start(f32[512]{0:T(512)} %param.13) | copy-start | bytes 6148
  7.2 151.0 %all-gather.5.cloned.1.call-start = ((), (), s32[]{:S(2)}) async-start(), calls=%async_computation | async-start | bytes 17039360 | tf_op jit(solution)/shard_map/all_gather | solution.py:22
  13.1 465.0 %all-gather.7.cloned.1.call-start = ((), (), s32[]{:S(2)}) async-start(), calls=%async_computation.1 | async-start | bytes 17039360 | tf_op jit(solution)/shard_map/all_gather | solution.py:22
Sparse Core Ops, SparseCore 0:
  13.2 144.9 all-gather.4
  176.2 283.9 all-gather.6
